TPU v7x, 512 devices: a whole 4x8x8 slice. The times are simulated.
512 devices in a mesh: tm: 64 (over y, x, z_lo), run: 8 (over z_hi, core).
Axes of the slice: x: 4, y: 8, z: 8 (z_hi: 4, z_lo: 2; z = z_hi * 2 + z_lo), core: 2. Of those that a mesh axis runs over, the one named last changes fastest.
Arguments:
- signal: bfloat16 [8, 65536, 256], P('run', 'tm'), may hold values from -6 to 6
- conv_weight: bfloat16 [768, 512], replicated, may hold values from -0.21875 to 0.21875
- conv_bias: float32 [512], replicated, may hold values from -3 to 3
- out_weight: bfloat16 [256, 256], replicated, may hold values from -0.375 to 0.375
- out_bias: float32 [256], replicated, may hold values from -3 to 3
- cotangent: bfloat16 [8, 65536, 256], P('run', 'tm'), may hold values from -8 to 8
Outputs:
- output: bfloat16 [8, 65536, 256], P('run', 'tm')
- grad_signal: bfloat16 [8, 65536, 256], P('run', 'tm')
- grad_conv_weight: float32 [768, 512], replicated
- grad_conv_bias: float32 [512], replicated
- grad_out_weight: float32 [256, 256], replicated
- grad_out_bias: float32 [256], replicated
All inputs are finite; a program needn't handle non-finite values.
Results may differ from a plain program's by a relative error of at most 0.0034.
Values may be sent and summed in bfloat16 or wider, within the bound.
A program may use at most 64 MiB of HBM per device.

v0:
```python
import jax
import jax.numpy as jnp
from jax import lax
from jax.sharding import PartitionSpec as P

DILATION_STEPS = 256
KERNEL_TAPS = 3


def passed_along(array, axis, by):
    size = lax.axis_size(axis)
    pairs = [(i, i + by) for i in range(size) if 0 <= i + by < size]
    return lax.ppermute(array, axis, pairs)


def local(signal, conv_weight, conv_bias, out_weight, out_bias, cotangent):
    device_rows = signal.shape[1]
    channels = signal.shape[2]
    receptive_span = (KERNEL_TAPS - 1) * DILATION_STEPS
    history = passed_along(signal[:, device_rows - receptive_span :, :], "tm", 1)
    padded_input = jnp.concatenate([history, signal], 1)
    tap_stack = jnp.concatenate(
        [
            padded_input[
                :,
                receptive_span
                - kernel_tap_index * DILATION_STEPS : receptive_span
                - kernel_tap_index * DILATION_STEPS
                + device_rows,
            ]
            for kernel_tap_index in range(KERNEL_TAPS)
        ],
        2,
    )
    preact = (
        jnp.einsum("bsk,kn->bsn", tap_stack, conv_weight, preferred_element_type=jnp.float32)
        + conv_bias
    )
    filtered = jnp.tanh(preact[..., :channels])
    gated = jax.nn.sigmoid(preact[..., channels:])
    mixed = (filtered * gated).astype(jnp.bfloat16)
    hidden = (
        jnp.einsum("bsc,cd->bsd", mixed, out_weight, preferred_element_type=jnp.float32) + out_bias
    )
    output = (signal.astype(jnp.float32) + hidden).astype(jnp.bfloat16)
    dmixed = jnp.einsum("bsd,cd->bsc", cotangent, out_weight, preferred_element_type=jnp.float32)
    dpre = jnp.concatenate(
        [dmixed * gated * (1.0 - filtered * filtered), dmixed * filtered * gated * (1.0 - gated)], 2
    ).astype(jnp.bfloat16)
    dstacked = jnp.einsum("bsn,kn->bsk", dpre, conv_weight, preferred_element_type=jnp.float32)
    local_grad = jnp.zeros((signal.shape[0], receptive_span + device_rows, channels), jnp.float32)
    for kernel_tap_index in range(KERNEL_TAPS):
        shifted_slice = dstacked[
            ..., kernel_tap_index * channels : (kernel_tap_index + 1) * channels
        ]
        local_grad = local_grad + jnp.pad(
            shifted_slice,
            (
                (0, 0),
                (
                    receptive_span - kernel_tap_index * DILATION_STEPS,
                    kernel_tap_index * DILATION_STEPS,
                ),
                (0, 0),
            ),
        )
    incoming = passed_along(local_grad[:, :receptive_span].astype(jnp.bfloat16), "tm", -1).astype(
        jnp.float32
    )
    grad_signal = (
        cotangent.astype(jnp.float32)
        + local_grad[:, receptive_span:]
        + jnp.pad(incoming, ((0, 0), (device_rows - receptive_span, 0), (0, 0)))
    )
    grad_signal = grad_signal.astype(jnp.bfloat16)
    grad_conv = jnp.einsum("bsk,bsn->kn", tap_stack, dpre, preferred_element_type=jnp.float32)
    grad_cbias = jnp.sum(dpre.astype(jnp.float32), (0, 1))
    grad_proj = jnp.einsum("bsc,bsd->cd", mixed, cotangent, preferred_element_type=jnp.float32)
    grad_pbias = jnp.sum(cotangent.astype(jnp.float32), (0, 1))
    scale = float(signal.shape[0] * lax.axis_size("run") * device_rows * lax.axis_size("tm")) ** (
        -0.5
    )
    summed = lax.psum((grad_conv, grad_cbias, grad_proj, grad_pbias), ("tm", "run"))
    return (
        output,
        grad_signal,
        summed[0] * scale,
        summed[1] * scale,
        summed[2] * scale,
        summed[3] * scale,
    )


def solution(mesh):
    placed = (P("run", "tm", None), P(), P(), P(), P(), P("run", "tm", None))
    return jax.shard_map(
        local,
        mesh=mesh,
        in_specs=placed,
        out_specs=(P("run", "tm", None), P("run", "tm", None), P(), P(), P(), P()),
        check_vma=False,
    )
```

profile of v0, /device:TPU:1, one launch (start us, length us, event | category | flops | bytes accessed | tf_op | source)
XLA Modules:
  0.0 329.9 jit_solution(11281328637928422365)
XLA Ops:
  7.2 0.0 copy-start
  7.2 0.0 copy-start.2
  7.2 0.0 all-reduce.8.cloned.1.call-start
  7.2 1.1 slice.31
  8.3 4.8 %collective-permute-start = (bf16[1,512,256]{2,1,0:T(8,128)(2,1)S(1)}, bf16[1,512,256]{2,1,0:T(8,128)(2,1)S(1)}, u32[]{:S(2)}, u32[]{:S(2)}) collective-permute-start(bf16[1,512,256]{2,1,0:T(8,128)(2,1)S(1)} %slice.31), channel_id=1, source_target_pairs={{0,8},{8,16},{16,24},{24,32},{32,40},{40,48},{48,56},{56,64},{64,7... | collective-permute-start | bytes 786440 | tf_op jit(solution)/shard_map/ppermute | solution.py:13
  13.2 3.3 collective-permute-done
  16.5 1.1 constant_dynamic-update-slice_fusion
  17.5 0.1 fusion.17
  17.7 0.0 copy-start.1
  17.7 0.0 copy-start.5
  17.7 1.0 add_bitcast_fusion
  18.7 0.8 multiply_convert_fusion.1
  19.5 0.0 copy-start.3
  19.5 0.2 convert_reduce_fusion
  19.8 2.2 fusion.8
  21.9 2.7 convolution_bitcast_fusion
  24.6 1.0 fusion.10
  25.6 2.1 fusion.16
  27.7 0.2 pad_add_fusion
  27.9 0.0 copy-start.7
  27.9 0.7 slice.74
  28.7 1.3 collective-permute-start.1
  30.0 0.0 all-reduce.8.cloned.1.call-update
  30.0 2.2 fusion.2
  32.2 4.4 %collective-permute-done.1 = bf16[1,512,256]{2,1,0:T(8,128)(2,1)} collective-permute-done((bf16[1,512,256]{2,1,0:T(8,128)(2,1)}, bf16[1,512,256]{2,1,0:T(8,128)(2,1)}, u32[]{:S(2)}, u32[]{:S(2)}) %collective-permute-start.1) | collective-permute-done | bytes 262176 | tf_op jit(solution)/shard_map/ppermute | solution.py:13
  36.6 2.0 convert_reduce_fusion.1
  38.6 113.1 %all-reduce.4 = (f32[512]{0:T(512)S(1)}, f32[256]{0:T(256)S(1)}) all-reduce(f32[512]{0:T(512)S(1)} %convert_reduce_fusion, f32[256]{0:T(256)S(1)} %get-tuple-element.18), channel_id=1, replica_groups=mesh['tm'=64,'run'=8] {'tm','run'}, use_global_device_ids=true, to_apply=%region_2.3 | all-reduce | flops 768 | bytes 6144 | tf_op jit(solution)/shard_map/psum | solution.py:83
  151.6 0.6 broadcast_multiply_fusion.3
  152.2 0.6 broadcast_multiply_fusion.2
  152.8 166.8 %all-reduce.8.cloned.1.call-done = (f32[768,512]{1,0:T(8,128)}, f32[256,256]{1,0:T(8,128)}) async-done(((f32[768,512]{1,0:T(8,128)}, f32[256,256]{1,0:T(8,128)}), (f32[768,512]{1,0:T(8,128)}, f32[256,256]{1,0:T(8,128)})) %all-reduce.8.cloned.1.call-update) | async-done | bytes 1835024 | tf_op jit(solution)/shard_map/psum | solution.py:83
  319.5 2.8 broadcast_multiply_fusion
  322.3 0.7 broadcast_multiply_fusion.1
  (11 shorter events, 0.0 us)
Async XLA Ops:
  7.2 10.5 %copy-start = (bf16[768,512]{1,0:T(8,128)(2,1)S(1)}, bf16[768,512]{1,0:T(8,128)(2,1)}, u32[]{:S(2)}) copy-start(bf16[768,512]{1,0:T(8,128)(2,1)} %param.7) | copy-start | bytes 2359300
  7.2 10.5 %copy-start.2 = (bf16[1,1024,256]{2,1,0:T(8,128)(2,1)S(1)}, bf16[1,1024,256]{2,1,0:T(8,128)(2,1)}, u32[]{:S(2)}) copy-start(bf16[1,1024,256]{2,1,0:T(8,128)(2,1)} %param.6) | copy-start | bytes 1572868
  7.2 10.5 %copy-start.6 = (f32[512]{0:T(512)S(1)}, f32[512]{0:T(512)}, u32[]{:S(2)}) copy-start(f32[512]{0:T(512)} %param.8) | copy-start | bytes 6148
  7.2 312.3 %all-reduce.8.cloned.1.call-start = ((), (), s32[]{:S(2)}) async-start(), calls=%async_computation | async-start | bytes 3670016 | tf_op jit(solution)/shard_map/psum | solution.py:83
  8.3 8.1 %collective-permute-start = (bf16[1,512,256]{2,1,0:T(8,128)(2,1)S(1)}, bf16[1,512,256]{2,1,0:T(8,128)(2,1)S(1)}, u32[]{:S(2)}, u32[]{:S(2)}) collective-permute-start(bf16[1,512,256]{2,1,0:T(8,128)(2,1)S(1)} %slice.31), channel_id=1, source_target_pairs={{0,8},{8,16},{16,24},{24,32},{32,40},{40,48},{48,56},{56,64},{64,7... | collective-permute-start | bytes 786440 | tf_op jit(solution)/shard_map/ppermute | solution.py:13
  17.7 1.1 copy-start.1
  17.7 1.1 copy-start.5
  19.5 5.1 %copy-start.3 = (bf16[1024,256]{0,1:T(8,128)(2,1)}, bf16[1024,256]{0,1:T(8,128)(2,1)S(1)}, u32[]{:S(2)}) copy-start(bf16[1024,256]{0,1:T(8,128)(2,1)S(1)} %get-tuple-element.15) | copy-start | bytes 1572868
  27.9 2.1 copy-start.7
  28.7 7.9 %collective-permute-start.1 = (bf16[1,512,256]{2,1,0:T(8,128)(2,1)}, bf16[1,512,256]{2,1,0:T(8,128)(2,1)}, u32[]{:S(2)}, u32[]{:S(2)}) collective-permute-start(bf16[1,512,256]{2,1,0:T(8,128)(2,1)} %slice.74), channel_id=1, source_target_pairs={{8,0},{16,8},{24,16},{32,24},{40,32},{48,40},{56,48},{64,56},{72,6... | collective-permute-start | bytes 786440 | tf_op jit(solution)/shard_map/ppermute | solution.py:13
  319.5 2.8 copy-start.4
Sparse Core Ops, SparseCore 0:
  30.1 289.3 all-reduce.7
where the time goes:
time: 330 us
  waiting for transfers between devices  174 us (53%)
  blocking collectives  113 us (34%)
  between operations  14.2 us (4%)
  matrix products  9.89 us (3%)
  other arithmetic  7.02 us (2%)
  starting transfers between devices  6.16 us (2%)
  local copies, waits for them, and re-layouts  5.08 us (2%)
    psum x1, waiting for transfers between devices, local(): lax.psum((grad_conv, grad_cbias, grad_proj, grad_pbias), ('tm', 'run'))  167 us
    psum x1, blocking collectives, local(): lax.psum((grad_conv, grad_cbias, grad_proj, grad_pbias), ('tm', 'run'))  113 us
    ppermute x2, waiting for transfers between devices, passed_along(): return lax.ppermute(array, axis, pairs)  7.68 us
  transfers between devices with their start and end apart: 3, of which 3 were waited for; matrix products, arithmetic and copies ran while one was open for 2% of the time, Pallas kernels for 0%

commit v1 on v0

v1 whole, which is shorter than its diff:
```python
import jax
import jax.numpy as jnp
from jax import lax
from jax.experimental import pallas as pl
from jax.experimental.pallas import tpu as pltpu
from jax.sharding import PartitionSpec as P

MESH = pl.DeviceIdType.MESH
BF = jnp.bfloat16
F32 = jnp.float32
NY, NX, NZ = 8, 4, 8
TM = 64
B = 256
CH = 4
PARTNERS = 32
HI, LO = 128, 136


def nt(a, b):
    return lax.dot_general(a, b, (((1,), (1,)), ((), ())), preferred_element_type=F32)


def tn(a, b):
    return lax.dot_general(a, b, (((0,), (0,)), ((), ())), preferred_element_type=F32)


def nn(a, b):
    return jnp.dot(a, b, preferred_element_type=F32)


def place(y, x, z, c):
    return {"tm": (y * NX + x) * 2 + z % 2, "run": (z // 2) * 2 + c}


def main_kernel(
    scale,
    sig, cw, cb, ow, ob, cot,
    out_ref, gs_ref, res_ref,
    sx, cv, wv, owv, cbv, obv, mixed, dp, grad, gpart, bsend, binc,
    sbuf, cbuf, acc, rbuf, part, agb, agc,
    in_sem, halo_s, halo_r, back_s, back_r,
    cs, cr, rs, rr, ps, pr, gsem, gr, s2, r2,
):
    tm, run = lax.axis_index("tm"), lax.axis_index("run")
    y, x, z, c = tm // 8, (tm // 2) % 4, (run // 2) * 2 + tm % 2, run % 2
    after = {"tm": (tm + 1) % TM, "run": run}
    before = {"tm": (tm + TM - 1) % TM, "run": run}
    sibling = place(y, x, z, 1 - c)

    def member(colour, o):
        if colour == 0:
            zz, xx = (z + o // 4) % NZ, (x + o) % NX
            return place(y, xx, zz, c), zz * 4 + xx
        yy, xx = (y + o // 4) % NY, (x + o) % NX
        return place(yy, xx, z, c), yy * 4 + xx

    def along(colour, o):
        return place((y + o) % NY, x, z, c) if colour == 0 else place(y, x, (z + o) % NZ, c)

    mine = (z * 4 + x, y * 4 + x)
    line = (y, z)

    def remote(src, dst, send, recv, device):
        return pltpu.make_async_remote_copy(
            src_ref=src, dst_ref=dst, send_sem=send, recv_sem=recv, device_id=device, device_id_type=MESH
        )

    def wait_bytes(ref, sem):
        pltpu.make_async_copy(ref, ref, sem).wait()

    loads = [
        pltpu.make_async_copy(sig.at[0], sx.at[pl.ds(2 * B, 4 * B)], in_sem.at[0]),
        pltpu.make_async_copy(cw, wv, in_sem.at[1]),
        pltpu.make_async_copy(cb, cbv, in_sem.at[2]),
        pltpu.make_async_copy(cot.at[0], cv, in_sem.at[3]),
        pltpu.make_async_copy(ow, owv, in_sem.at[4]),
        pltpu.make_async_copy(ob, obv, in_sem.at[5]),
    ]
    for load in loads:
        load.start()

    barrier = pltpu.get_barrier_semaphore()

    def announce(o, carry):
        for colour in range(2):
            pl.semaphore_signal(barrier, inc=1, device_id=member(colour, o)[0], device_id_type=MESH)
        return carry

    lax.fori_loop(1, PARTNERS, announce, 0)
    for device in (after, before, sibling):
        pl.semaphore_signal(barrier, inc=1, device_id=device, device_id_type=MESH)
    for load in loads:
        load.wait()

    def rows(b):
        return pl.ds(b * B, B)

    def activate(b):
        pre = (
            nn(sx[(b + 2) * B : (b + 3) * B], wv[0:B])
            + nn(sx[(b + 1) * B : (b + 2) * B], wv[B : 2 * B])
            + nn(sx[b * B : (b + 1) * B], wv[2 * B : 3 * B])
            + cbv[...]
        )
        f = jnp.tanh(pre[:, :B])
        g = 0.5 * jnp.tanh(0.5 * pre[:, B:]) + 0.5
        mixed[rows(b), :] = (f * g).astype(BF)
        dm = nt(cv[rows(b), :], owv[...])
        dmg = dm * g
        dp[rows(b), 0:B] = (dmg * (1.0 - f * f)).astype(BF)
        dp[rows(b), B : 2 * B] = (dmg * f * (1.0 - g)).astype(BF)

    def tap_term(k, b, n):
        return tn(sx[(b + 2 - k) * B : (b + 2 - k + n) * B], dp[b * B : (b + n) * B])

    def out_term(b, n):
        return tn(mixed[b * B : (b + n) * B], cv[b * B : (b + n) * B])

    def bias_terms(b, n):
        d = jnp.sum(dp[b * B : (b + n) * B].astype(F32), 0, keepdims=True)
        o = jnp.sum(cv[b * B : (b + n) * B].astype(F32), 0, keepdims=True)
        return d, o

    def back(b, k):
        return nt(dp[rows(b), :], wv[k * B : (k + 1) * B])

    def emit_output(b):
        h = nn(mixed[rows(b), :], owv[...]) + obv[...]
        out_ref[rows(b), :] = (sx[(b + 2) * B : (b + 3) * B].astype(F32) + h).astype(BF)

    activate(2)
    pl.semaphore_wait(barrier, 2 * (PARTNERS - 1) + 3)
    halos = []
    for i in (1, 0):
        copy = remote(sx.at[pl.ds((4 + i) * B, B)], sx.at[pl.ds(i * B, B)], halo_s.at[i], halo_r.at[i], after)
        copy.start()
        halos.append(copy)

    activate(3)
    grad[:, 3, HI:B, :] = jnp.zeros((2, B - HI, B), F32)
    for k in range(3):
        t = tap_term(k, 2, 2)
        grad[0, k] = t[:, :B]
        grad[1, k] = t[:, B:]
    t = out_term(2, 2)
    grad[0, 3, 0:HI, :] = t[:HI]
    grad[1, 3, 0:HI, :] = t[HI:]
    d23, o23 = bias_terms(2, 2)
    gpart[0:B, :] = cv[rows(2), :].astype(F32) + back(2, 0) + back(3, 1)
    gpart[B : 2 * B, :] = cv[rows(3), :].astype(F32) + back(3, 0)
    emit_output(2)
    emit_output(3)

    first = tm == 0

    halos[0].wait_recv()

    @pl.when(first)
    def _():
        sx[B : 2 * B, :] = jnp.zeros((B, B), BF)

    activate(1)
    for k in range(3):
        t = tap_term(k, 1, 1)
        grad[0, k] += t[:, :B]
        grad[1, k] += t[:, B:]
    t = out_term(1, 1)
    grad[0, 3, 0:HI, :] += t[:HI]
    grad[1, 3, 0:HI, :] += t[HI:]

    halos[1].wait_recv()

    @pl.when(first)
    def _():
        sx[0:B, :] = jnp.zeros((B, B), BF)

    activate(0)
    pair = []

    def send_half(k):
        copy = remote(sbuf.at[k], cbuf.at[k], cs.at[k], cr.at[k], sibling)
        copy.start()
        pair.append(copy)

    for k in range(3):
        t = tap_term(k, 0, 1)
        grad[0, k] += t[:, :B]
        grad[1, k] += t[:, B:]
        sbuf[k] = grad[1 - c, k].astype(BF)
        send_half(k)
    t = out_term(0, 1)
    grad[0, 3, 0:HI, :] += t[:HI]
    grad[1, 3, 0:HI, :] += t[HI:]
    d01, o01 = bias_terms(0, 2)
    d, o = d23 + d01, o23 + o01
    for h in range(2):
        grad[h, 3, HI : HI + 1, :] = d[:, h * B : (h + 1) * B]
        grad[h, 3, HI + 1 : HI + 2, :] = o
    sbuf[3] = grad[1 - c, 3].astype(BF)
    bias = grad[1 - c, 3, HI:LO, :]
    low = bias - bias.astype(BF).astype(F32)
    sbuf[3, LO : LO + 8, :] = low.astype(BF)
    send_half(3)

    for k in range(CH):
        pair[k].wait_recv()
        s = grad[c, k] + cbuf[k].astype(F32)
        r = s.astype(BF)
        acc[k, 0] = s[:, :128].reshape(PARTNERS, 8, 128).astype(BF)
        acc[k, 1] = s[:, 128:].reshape(PARTNERS, 8, 128).astype(BF)
        if k == 3:
            t = s[HI:LO] + s[LO : LO + 8]
            high = t.astype(BF)
            low = (t - high.astype(F32)).astype(BF)
            for colour in range(2):
                acc[k, colour, HI // 8] = high[:, colour * 128 : (colour + 1) * 128]
                acc[k, colour, LO // 8] = low[:, colour * 128 : (colour + 1) * 128]

        def scatter(o, carry):
            for colour in range(2):
                device, p = member(colour, o)
                remote(acc.at[k, colour, p], rbuf.at[k, colour, o], rs.at[k], rr.at[k, colour], device).start()
            return carry

        lax.fori_loop(1, PARTNERS, scatter, 0)

    bsend[0:B, :] = back(0, 2).astype(BF)
    bsend[B : 2 * B, :] = (back(0, 1) + back(1, 2)).astype(BF)
    backward = remote(bsend, binc, back_s, back_r, before)
    backward.start()
    gs_ref[rows(0), :] = (cv[rows(0), :].astype(F32) + back(0, 0) + back(1, 1) + back(2, 2)).astype(BF)
    gs_ref[rows(1), :] = (cv[rows(1), :].astype(F32) + back(1, 0) + back(2, 1) + back(3, 2)).astype(BF)
    emit_output(0)
    emit_output(1)

    for k in range(CH):
        for colour in range(2):
            wait_bytes(rbuf.at[k, colour, pl.ds(1, PARTNERS - 1)], rr.at[k, colour])
            s = acc[k, colour, mine[colour]].astype(F32)
            s = s + jnp.sum(rbuf[k, colour, 1:PARTNERS].astype(F32), 0)
            part[k, colour, line[colour]] = s

            def spread(o, carry):
                ref = part.at[k, colour, line[colour]]
                remote(ref, ref, ps.at[k], pr.at[k, colour], along(colour, o)).start()
                return carry

            lax.fori_loop(1, 8, spread, 0)

    for k in range(CH):
        for colour in range(2):
            wait_bytes(part.at[k, colour, pl.ds(1, 7)], pr.at[k, colour])
            t = part[k, colour, 0]
            for i in range(1, 8):
                t = t + part[k, colour, i]
            agb[k, colour, mine[colour]] = t.astype(BF)

            def gather(o, carry):
                ref = agb.at[k, colour, mine[colour]]
                remote(ref, ref, gsem.at[k], gr.at[k, colour], member(colour, o)[0]).start()
                return carry

            lax.fori_loop(1, PARTNERS, gather, 0)

    backward.wait_recv()
    last = tm == TM - 1

    @pl.when(last)
    def _():
        binc[...] = jnp.zeros((2 * B, B), BF)

    for i in range(2):
        gs_ref[rows(2 + i), :] = (gpart[rows(i), :] + binc[rows(i), :].astype(F32)).astype(BF)

    swap = []
    for k in range(CH):
        for colour in range(2):
            wait_bytes(agb.at[k, colour, pl.ds(1, PARTNERS - 1)], gr.at[k, colour])
        copy = remote(agb.at[k], agc.at[k], s2.at[k], r2.at[k], sibling)
        copy.start()
        swap.append(copy)
        for colour in range(2):
            v = agb[k, colour].astype(F32).reshape(B, 128) * scale
            res_ref[c, pl.ds(k * B, B), colour * 128 : (colour + 1) * 128] = v
    for k in range(CH):
        swap[k].wait_recv()
        for colour in range(2):
            v = agc[k, colour].astype(F32).reshape(B, 128) * scale
            res_ref[1 - c, pl.ds(k * B, B), colour * 128 : (colour + 1) * 128] = v

    for copy in (*halos, *pair, backward, *swap):
        copy.wait_send()
    for k in range(CH):
        wait_bytes(rbuf.at[k, :, pl.ds(1, PARTNERS - 1)], rs.at[k])
        wait_bytes(part.at[k, :, pl.ds(1, 7)], ps.at[k])
        wait_bytes(agb.at[k, :, pl.ds(1, PARTNERS - 1)], gsem.at[k])


def write_kernel(out, gs, res, out_ref, gs_ref, gcw_ref, gcb_ref, gow_ref, gob_ref, sem):
    copies = [
        pltpu.make_async_copy(out, out_ref.at[0], sem.at[0]),
        pltpu.make_async_copy(gs, gs_ref.at[0], sem.at[1]),
        pltpu.make_async_copy(res.at[0, pl.ds(0, 768)], gcw_ref.at[:, pl.ds(0, B)], sem.at[2]),
        pltpu.make_async_copy(res.at[1, pl.ds(0, 768)], gcw_ref.at[:, pl.ds(B, B)], sem.at[3]),
        pltpu.make_async_copy(res.at[0, pl.ds(768, 128)], gow_ref.at[pl.ds(0, 128)], sem.at[4]),
        pltpu.make_async_copy(res.at[1, pl.ds(768, 128)], gow_ref.at[pl.ds(128, 128)], sem.at[5]),
    ]
    for copy in copies:
        copy.start()
    hi, lo = 768 + HI, 768 + LO
    for h in range(2):
        gcb_ref[0:1, h * B : (h + 1) * B] = res[h, hi : hi + 1, :] + res[h, lo : lo + 1, :]
    gob_ref[...] = res[0, hi + 1 : hi + 2, :] + res[0, lo + 1 : lo + 2, :]
    for copy in copies:
        copy.wait()


def local(signal, conv_weight, conv_bias, out_weight, out_bias, cotangent):
    any_space = pl.BlockSpec(memory_space=pl.ANY)
    vmem = pl.BlockSpec(memory_space=pltpu.VMEM)
    dma = pltpu.SemaphoreType.DMA
    scale = float(8 * 65536) ** -0.5

    def kernel(*refs):
        main_kernel(scale, *refs)

    out, gs, res = pl.pallas_call(
        kernel,
        out_shape=(pltpu.VMEM((4 * B, B), BF), pltpu.VMEM((4 * B, B), BF), pltpu.VMEM((2, CH * B, B), F32)),
        in_specs=[any_space] * 6,
        out_specs=[vmem] * 3,
        scratch_shapes=[
            pltpu.VMEM((6 * B, B), BF),
            pltpu.VMEM((4 * B, B), BF),
            pltpu.VMEM((3 * B, 2 * B), BF),
            pltpu.VMEM((B, B), BF),
            pltpu.VMEM((1, 2 * B), F32),
            pltpu.VMEM((1, B), F32),
            pltpu.VMEM((4 * B, B), BF),
            pltpu.VMEM((4 * B, 2 * B), BF),
            pltpu.VMEM((2, CH, B, B), F32),
            pltpu.VMEM((2 * B, B), F32),
            pltpu.VMEM((2 * B, B), BF),
            pltpu.VMEM((2 * B, B), BF),
            pltpu.VMEM((CH, B, B), BF),
            pltpu.VMEM((CH, B, B), BF),
            pltpu.VMEM((CH, 2, PARTNERS, 8, 128), BF),
            pltpu.VMEM((CH, 2, PARTNERS, 8, 128), BF),
            pltpu.VMEM((CH, 2, 8, 8, 128), F32),
            pltpu.VMEM((CH, 2, PARTNERS, 8, 128), BF),
            pltpu.VMEM((CH, 2, PARTNERS, 8, 128), BF),
            dma((6,)),
            dma((2,)),
            dma((2,)),
            dma,
            dma,
            dma((CH,)),
            dma((CH,)),
            dma((CH,)),
            dma((CH, 2)),
            dma((CH,)),
            dma((CH, 2)),
            dma((CH,)),
            dma((CH, 2)),
            dma((CH,)),
            dma((CH,)),
        ],
        compiler_params=pltpu.CompilerParams(
            collective_id=0, has_side_effects=True, vmem_limit_bytes=40 * 1024 * 1024
        ),
        name="block",
    )(signal, conv_weight, conv_bias.reshape(1, -1), out_weight, out_bias.reshape(1, -1), cotangent)
    output, grad_signal, gcw, gcb, gow, gob = pl.pallas_call(
        write_kernel,
        out_shape=(
            jax.ShapeDtypeStruct((1, 4 * B, B), BF),
            jax.ShapeDtypeStruct((1, 4 * B, B), BF),
            jax.ShapeDtypeStruct((3 * B, 2 * B), F32),
            jax.ShapeDtypeStruct((1, 2 * B), F32),
            jax.ShapeDtypeStruct((B, B), F32),
            jax.ShapeDtypeStruct((1, B), F32),
        ),
        in_specs=[vmem] * 3,
        out_specs=[any_space, any_space, any_space, vmem, any_space, vmem],
        scratch_shapes=[dma((6,))],
        name="write",
    )(out, gs, res)
    return output, grad_signal, gcw, gcb.reshape(-1), gow, gob.reshape(-1)


def solution(mesh):
    placed = (P("run", "tm", None), P(), P(), P(), P(), P("run", "tm", None))
    return jax.shard_map(
        local,
        mesh=mesh,
        in_specs=placed,
        out_specs=(P("run", "tm", None), P("run", "tm", None), P(), P(), P(), P()),
        check_vma=False,
    )
```

time: 330 us -> 72.9 us (0.22)
  waiting for transfers between devices: 174 us -> 0 us
  blocking collectives: 113 us -> 0 us
  Pallas kernels: 0 us -> 63.5 us
  between operations: 14.2 us -> 0.67 us
  matrix products: 9.89 us -> 0 us
  other arithmetic: 7.02 us -> 0 us
  starting transfers between devices: 6.16 us -> 0 us
  local copies, waits for them, and re-layouts: 5.08 us -> 8.4 us
    psum x1 -> x0, waiting for transfers between devices: 167 us -> none  [local(): lax.psum((grad_conv, grad_cbias, grad_proj, grad_pbias), ('tm', 'run'))]
    psum x1 -> x0, blocking collectives: 113 us -> none  [local(): lax.psum((grad_conv, grad_cbias, grad_proj, grad_pbias), ('tm', 'run'))]
    pallas_call x0 -> x2, Pallas kernels: none -> 63.5 us  [the longest x1 59.3 us: local(): pl.pallas_call(kernel, out_shape=(pltpu.VMEM((4 * B, B), BF), pltpu.VMEM(...]
    dot_general x6 -> x0, matrix products: 9.89 us -> none  [the longest x1 2.68 us: local(): jnp.einsum('bsn,kn->bsk', dpre, conv_weight, preferred_element_type=jnp.f...]
    unnamed x17 -> x18, local copies, waits for them, and re-layouts: 0.07 us -> 8.4 us
    ppermute x2 -> x0, waiting for transfers between devices: 7.68 us -> none  [passed_along(): return lax.ppermute(array, axis, pairs)]
    ppermute x2 -> x0, starting transfers between devices: 6.12 us -> none  [passed_along(): return lax.ppermute(array, axis, pairs)]
    mul x4 -> x0, other arithmetic: 4.64 us -> none  [the longest x1 2.77 us: local(): summed[0] * scale]
  transfers between devices with their start and end apart: 3 -> 0, of which waited for: 3 -> 0; matrix products, arithmetic and copies ran while one was open for 2% -> 0% of each run, Pallas kernels for 0% -> 0%
where the time goes in v1:
time: 72.9 us; the launch traced here: 72.5 us
  Pallas kernels  63.5 us (87%)
  local copies, waits for them, and re-layouts  8.4 us (12%)
    pallas_call x1, Pallas kernels, local(): pl.pallas_call(kernel, out_shape=(pltpu.VMEM((4 * B, B), BF), pltpu.VMEM(...  59.3 us
    unnamed x18, local copies, waits for them, and re-layouts  8.4 us
    pallas_call x1, Pallas kernels, local(): pl.pallas_call(write_kernel, out_shape=(jax.ShapeDtypeStruct((1, 4 * B, B...  4.12 us

profile of v1, /device:TPU:1, one launch (start us, length us, event | category | flops | bytes accessed | tf_op | source)
XLA Modules:
  0.0 72.5 jit_solution(8957312592898457060)
XLA Ops:
  0.6 0.0 copy-start.1
  0.6 1.1 %copy-done.1 = bf16[768,512]{1,0:T(8,128)(2,1)S(1)} copy-done((bf16[768,512]{1,0:T(8,128)(2,1)S(1)}, bf16[768,512]{1,0:T(8,128)(2,1)}, u32[]{:S(2)}) %copy-start.1) | copy-done | bytes 786456
  1.8 0.0 copy-start.2
  1.8 1.0 %copy-done.2 = bf16[1,1024,256]{2,1,0:T(8,128)(2,1)S(1)} copy-done((bf16[1,1024,256]{2,1,0:T(8,128)(2,1)S(1)}, bf16[1,1024,256]{2,1,0:T(8,128)(2,1)}, u32[]{:S(2)}) %copy-start.2) | copy-done | bytes 524312
  2.8 0.0 copy-start.3
  2.8 1.0 %copy-done.3 = bf16[1,1024,256]{2,1,0:T(8,128)(2,1)S(1)} copy-done((bf16[1,1024,256]{2,1,0:T(8,128)(2,1)S(1)}, bf16[1,1024,256]{2,1,0:T(8,128)(2,1)}, u32[]{:S(2)}) %copy-start.3) | copy-done | bytes 524312
  3.9 0.0 copy-start.6
  3.9 0.9 %copy-done.6 = bf16[256,256]{1,0:T(8,128)(2,1)S(1)} copy-done((bf16[256,256]{1,0:T(8,128)(2,1)S(1)}, bf16[256,256]{1,0:T(8,128)(2,1)}, u32[]{:S(2)}) %copy-start.6) | copy-done | bytes 131096
  4.8 0.0 copy-start.7
  4.8 0.7 copy-done.7
  5.4 0.0 copy-start.8
  5.4 0.7 copy-done.8
  6.1 59.3 %block.1 = (bf16[1024,256]{1,0:T(8,128)(2,1)S(1)}, bf16[1024,256]{1,0:T(8,128)(2,1)S(1)}, f32[2,1024,256]{2,1,0:T(8,128)S(1)}) custom-call(bf16[1,1024,256]{2,1,0:T(8,128)(2,1)S(1)} %copy-done.2, bf16[768,512]{1,0:T(8,128)(2,1)S(1)} %copy-done.1, f32[1,512]{1,0:T(1,128)S(1)} %bitcast.4, bf16[256,256]{1,0:T(8,128)(2,1)S(1)} %copy-done.6, ...), custom_call_target="tpu_custom_call" | custom-call | tf_op jit(solution)/shard_map/block/pallas_call | solution.py:327
  65.5 0.0 copy-start
  65.5 1.3 %copy-done = f32[2,1024,256]{2,1,0:T(8,128)} copy-done((f32[2,1024,256]{2,1,0:T(8,128)}, f32[2,1024,256]{2,1,0:T(8,128)S(1)}, u32[]{:S(2)}) %copy-start) | copy-done | bytes 2097176
  66.8 0.0 copy-start.4
  66.8 0.8 %copy-done.4 = bf16[1024,256]{1,0:T(8,128)(2,1)} copy-done((bf16[1024,256]{1,0:T(8,128)(2,1)}, bf16[1024,256]{1,0:T(8,128)(2,1)S(1)}, u32[]{:S(2)}) %copy-start.4) | copy-done | bytes 524312
  67.6 0.0 copy-start.5
  67.6 0.8 %copy-done.5 = bf16[1024,256]{1,0:T(8,128)(2,1)} copy-done((bf16[1024,256]{1,0:T(8,128)(2,1)}, bf16[1024,256]{1,0:T(8,128)(2,1)S(1)}, u32[]{:S(2)}) %copy-start.5) | copy-done | bytes 524312
  68.4 4.1 %write.1 = (bf16[1,1024,256]{2,1,0:T(8,128)(2,1)}, bf16[1,1024,256]{2,1,0:T(8,128)(2,1)}, f32[768,512]{1,0:T(8,128)}, f32[1,512]{1,0:T(1,128)}, f32[256,256]{1,0:T(8,128)}, /*index=5*/f32[1,256]{1,0:T(1,128)}) custom-call(bf16[1024,256]{1,0:T(8,128)(2,1)} %copy-done.4, bf16[1024,256]{1,0:T(8,128)(2,1)} %copy-done.5, f32[2,1024,256]{2,1,0:T(8,128)} %copy-done), custom_call_target="tpu_custom_call" | custom-call | tf_op jit(solution)/shard_map/write/pallas_call | solution.py:373
Async XLA Ops:
  0.6 1.1 %copy-start.1 = (bf16[768,512]{1,0:T(8,128)(2,1)S(1)}, bf16[768,512]{1,0:T(8,128)(2,1)}, u32[]{:S(2)}) copy-start(bf16[768,512]{1,0:T(8,128)(2,1)} %refs_1_.1) | copy-start | bytes 2359300
  1.8 1.0 %copy-start.2 = (bf16[1,1024,256]{2,1,0:T(8,128)(2,1)S(1)}, bf16[1,1024,256]{2,1,0:T(8,128)(2,1)}, u32[]{:S(2)}) copy-start(bf16[1,1024,256]{2,1,0:T(8,128)(2,1)} %refs_0_.1) | copy-start | bytes 1572868
  2.8 1.0 %copy-start.3 = (bf16[1,1024,256]{2,1,0:T(8,128)(2,1)S(1)}, bf16[1,1024,256]{2,1,0:T(8,128)(2,1)}, u32[]{:S(2)}) copy-start(bf16[1,1024,256]{2,1,0:T(8,128)(2,1)} %refs_5_.1) | copy-start | bytes 1572868
  3.9 0.9 %copy-start.6 = (bf16[256,256]{1,0:T(8,128)(2,1)S(1)}, bf16[256,256]{1,0:T(8,128)(2,1)}, u32[]{:S(2)}) copy-start(bf16[256,256]{1,0:T(8,128)(2,1)} %refs_3_.1) | copy-start | bytes 393220
  4.8 0.7 copy-start.7
  5.4 0.7 copy-start.8
  65.5 1.3 %copy-start = (f32[2,1024,256]{2,1,0:T(8,128)}, f32[2,1024,256]{2,1,0:T(8,128)S(1)}, u32[]{:S(2)}) copy-start(f32[2,1024,256]{2,1,0:T(8,128)S(1)} %get-tuple-element.17.res) | copy-start | bytes 6291460
  66.8 0.8 %copy-start.4 = (bf16[1024,256]{1,0:T(8,128)(2,1)}, bf16[1024,256]{1,0:T(8,128)(2,1)S(1)}, u32[]{:S(2)}) copy-start(bf16[1024,256]{1,0:T(8,128)(2,1)S(1)} %get-tuple-element.15.out) | copy-start | bytes 1572868
  67.6 0.8 %copy-start.5 = (bf16[1024,256]{1,0:T(8,128)(2,1)}, bf16[1024,256]{1,0:T(8,128)(2,1)S(1)}, u32[]{:S(2)}) copy-start(bf16[1024,256]{1,0:T(8,128)(2,1)S(1)} %get-tuple-element.16.gs) | copy-start | bytes 1572868

commit v2 on v1

--- a/solution.py
+++ b/solution.py
@@ -28,8 +28,17 @@
     return jnp.dot(a, b, preferred_element_type=F32)
 
 
+def rem(a, n):
+    return lax.rem(a, jnp.int32(n))
+
+
+def div(a, n):
+    return lax.div(a, jnp.int32(n))
+
+
 def place(y, x, z, c):
-    return {"tm": (y * NX + x) * 2 + z % 2, "run": (z // 2) * 2 + c}
+    low = rem(z, 2)
+    return {"tm": (y * NX + x) * 2 + low, "run": z - low + c}
 
 
 def main_kernel(
@@ -42,20 +51,31 @@
     cs, cr, rs, rr, ps, pr, gsem, gr, s2, r2,
 ):
     tm, run = lax.axis_index("tm"), lax.axis_index("run")
-    y, x, z, c = tm // 8, (tm // 2) % 4, (run // 2) * 2 + tm % 2, run % 2
-    after = {"tm": (tm + 1) % TM, "run": run}
-    before = {"tm": (tm + TM - 1) % TM, "run": run}
+    c = rem(run, 2)
+    y, x, z = div(tm, 8), rem(div(tm, 2), NX), div(run, 2) * 2 + rem(tm, 2)
+    after = {"tm": rem(tm + 1, TM), "run": run}
+    before = {"tm": rem(tm + TM - 1, TM), "run": run}
     sibling = place(y, x, z, 1 - c)
 
-    def member(colour, o):
-        if colour == 0:
-            zz, xx = (z + o // 4) % NZ, (x + o) % NX
-            return place(y, xx, zz, c), zz * 4 + xx
-        yy, xx = (y + o // 4) % NY, (x + o) % NX
-        return place(yy, xx, z, c), yy * 4 + xx
+    columns = tuple(rem(x + i, NX) for i in range(NX))
 
     def along(colour, o):
-        return place((y + o) % NY, x, z, c) if colour == 0 else place(y, x, (z + o) % NZ, c)
+        return place(rem(y + o, NY), x, z, c) if colour == 0 else place(y, x, rem(z + o, NZ), c)
+
+    def plane(visit):
+        def line_of(i, first):
+            zz, yy = rem(z + i, NZ), rem(y + i, NY)
+            for j in range(first, NX):
+                xx = columns[j]
+                visit(0, i * NX + j, place(y, xx, zz, c), zz * NX + xx)
+                visit(1, i * NX + j, place(yy, xx, z, c), yy * NX + xx)
+
+        def step(i, carry):
+            line_of(i, 0)
+            return carry
+
+        lax.fori_loop(1, 8, step, 0)
+        line_of(0, 1)
 
     mine = (z * 4 + x, y * 4 + x)
     line = (y, z)
@@ -81,14 +101,16 @@
 
     barrier = pltpu.get_barrier_semaphore()
 
-    def announce(o, carry):
-        for colour in range(2):
-            pl.semaphore_signal(barrier, inc=1, device_id=member(colour, o)[0], device_id_type=MESH)
-        return carry
-
-    lax.fori_loop(1, PARTNERS, announce, 0)
     for device in (after, before, sibling):
         pl.semaphore_signal(barrier, inc=1, device_id=device, device_id_type=MESH)
+    plane(lambda colour, slot, device, p: pl.semaphore_signal(barrier, inc=1, device_id=device, device_id_type=MESH))
+    pl.semaphore_wait(barrier, 2 * (PARTNERS - 1) + 3)
+    halos = []
+    for i in (1, 0):
+        src = sig.at[0, pl.ds((2 + i) * B, B)]
+        copy = remote(src, sx.at[pl.ds(i * B, B)], halo_s.at[i], halo_r.at[i], after)
+        copy.start()
+        halos.append(copy)
     for load in loads:
         load.wait()
 
@@ -129,13 +151,6 @@
         out_ref[rows(b), :] = (sx[(b + 2) * B : (b + 3) * B].astype(F32) + h).astype(BF)
 
     activate(2)
-    pl.semaphore_wait(barrier, 2 * (PARTNERS - 1) + 3)
-    halos = []
-    for i in (1, 0):
-        copy = remote(sx.at[pl.ds((4 + i) * B, B)], sx.at[pl.ds(i * B, B)], halo_s.at[i], halo_r.at[i], after)
-        copy.start()
-        halos.append(copy)
-
     activate(3)
     grad[:, 3, HI:B, :] = jnp.zeros((2, B - HI, B), F32)
     for k in range(3):
@@ -205,7 +220,6 @@
     for k in range(CH):
         pair[k].wait_recv()
         s = grad[c, k] + cbuf[k].astype(F32)
-        r = s.astype(BF)
         acc[k, 0] = s[:, :128].reshape(PARTNERS, 8, 128).astype(BF)
         acc[k, 1] = s[:, 128:].reshape(PARTNERS, 8, 128).astype(BF)
         if k == 3:
@@ -216,18 +230,18 @@
                 acc[k, colour, HI // 8] = high[:, colour * 128 : (colour + 1) * 128]
                 acc[k, colour, LO // 8] = low[:, colour * 128 : (colour + 1) * 128]
 
-        def scatter(o, carry):
-            for colour in range(2):
-                device, p = member(colour, o)
-                remote(acc.at[k, colour, p], rbuf.at[k, colour, o], rs.at[k], rr.at[k, colour], device).start()
-            return carry
-
-        lax.fori_loop(1, PARTNERS, scatter, 0)
+        plane(
+            lambda colour, slot, device, p: remote(
+                acc.at[k, colour, p], rbuf.at[k, colour, slot], rs.at[k], rr.at[k, colour], device
+            ).start()
+        )
 
     bsend[0:B, :] = back(0, 2).astype(BF)
     bsend[B : 2 * B, :] = (back(0, 1) + back(1, 2)).astype(BF)
-    backward = remote(bsend, binc, back_s, back_r, before)
-    backward.start()
+    backward = [
+        remote(bsend.at[pl.ds(i * 128, 128)], binc.at[pl.ds(i * 128, 128)], back_s.at[i], back_r.at[i], before)
+        for i in range(CH)
+    ]
     gs_ref[rows(0), :] = (cv[rows(0), :].astype(F32) + back(0, 0) + back(1, 1) + back(2, 2)).astype(BF)
     gs_ref[rows(1), :] = (cv[rows(1), :].astype(F32) + back(1, 0) + back(2, 1) + back(3, 2)).astype(BF)
     emit_output(0)
@@ -246,6 +260,7 @@
                 return carry
 
             lax.fori_loop(1, 8, spread, 0)
+        backward[k].start()
 
     for k in range(CH):
         for colour in range(2):
@@ -255,40 +270,41 @@
                 t = t + part[k, colour, i]
             agb[k, colour, mine[colour]] = t.astype(BF)
 
-            def gather(o, carry):
-                ref = agb.at[k, colour, mine[colour]]
-                remote(ref, ref, gsem.at[k], gr.at[k, colour], member(colour, o)[0]).start()
-                return carry
-
-            lax.fori_loop(1, PARTNERS, gather, 0)
-
-    backward.wait_recv()
-    last = tm == TM - 1
-
-    @pl.when(last)
+        def gather(colour, slot, device, p):
+            ref = agb.at[k, colour, mine[colour]]
+            remote(ref, ref, gsem.at[k], gr.at[k, colour], device).start()
+
+        plane(gather)
+
+    def keep(h, k, colour, ref):
+        v = ref[k, colour].astype(F32).reshape(B, 128) * scale
+        res_ref[h, pl.ds(k * B, B), colour * 128 : (colour + 1) * 128] = v
+
+    swap = []
+    for k in range(CH):
+        for colour in range(2):
+            wait_bytes(agb.at[k, colour, pl.ds(1, PARTNERS - 1)], gr.at[k, colour])
+            copy = remote(agb.at[k, colour], agc.at[k, colour], s2.at[k, colour], r2.at[k, colour], sibling)
+            copy.start()
+            swap.append(copy)
+        for colour in range(2):
+            keep(c, k, colour, agb)
+
+    for copy in backward:
+        copy.wait_recv()
+
+    @pl.when(tm == TM - 1)
     def _():
         binc[...] = jnp.zeros((2 * B, B), BF)
 
     for i in range(2):
         gs_ref[rows(2 + i), :] = (gpart[rows(i), :] + binc[rows(i), :].astype(F32)).astype(BF)
-
-    swap = []
     for k in range(CH):
         for colour in range(2):
-            wait_bytes(agb.at[k, colour, pl.ds(1, PARTNERS - 1)], gr.at[k, colour])
-        copy = remote(agb.at[k], agc.at[k], s2.at[k], r2.at[k], sibling)
-        copy.start()
-        swap.append(copy)
-        for colour in range(2):
-            v = agb[k, colour].astype(F32).reshape(B, 128) * scale
-            res_ref[c, pl.ds(k * B, B), colour * 128 : (colour + 1) * 128] = v
-    for k in range(CH):
-        swap[k].wait_recv()
-        for colour in range(2):
-            v = agc[k, colour].astype(F32).reshape(B, 128) * scale
-            res_ref[1 - c, pl.ds(k * B, B), colour * 128 : (colour + 1) * 128] = v
-
-    for copy in (*halos, *pair, backward, *swap):
+            swap[2 * k + colour].wait_recv()
+            keep(1 - c, k, colour, agc)
+
+    for copy in (*halos, *pair, *backward, *swap):
         copy.wait_send()
     for k in range(CH):
         wait_bytes(rbuf.at[k, :, pl.ds(1, PARTNERS - 1)], rs.at[k])
@@ -324,7 +340,8 @@
     def kernel(*refs):
         main_kernel(scale, *refs)
 
-    out, gs, res = pl.pallas_call(
+    given = (signal, conv_weight, conv_bias.reshape(1, -1), out_weight, out_bias.reshape(1, -1), cotangent)
+    made = pl.pallas_call(
         kernel,
         out_shape=(pltpu.VMEM((4 * B, B), BF), pltpu.VMEM((4 * B, B), BF), pltpu.VMEM((2, CH * B, B), F32)),
         in_specs=[any_space] * 6,
@@ -352,8 +369,8 @@
             dma((6,)),
             dma((2,)),
             dma((2,)),
-            dma,
-            dma,
+            dma((CH,)),
+            dma((CH,)),
             dma((CH,)),
             dma((CH,)),
             dma((CH,)),
@@ -362,14 +379,14 @@
             dma((CH, 2)),
             dma((CH,)),
             dma((CH, 2)),
-            dma((CH,)),
-            dma((CH,)),
+            dma((CH, 2)),
+            dma((CH, 2)),
         ],
         compiler_params=pltpu.CompilerParams(
             collective_id=0, has_side_effects=True, vmem_limit_bytes=40 * 1024 * 1024
         ),
         name="block",
-    )(signal, conv_weight, conv_bias.reshape(1, -1), out_weight, out_bias.reshape(1, -1), cotangent)
+    )(*(pltpu.with_memory_space_constraint(v, pltpu.HBM) for v in given))
     output, grad_signal, gcw, gcb, gow, gob = pl.pallas_call(
         write_kernel,
         out_shape=(
@@ -384,7 +401,7 @@
         out_specs=[any_space, any_space, any_space, vmem, any_space, vmem],
         scratch_shapes=[dma((6,))],
         name="write",
-    )(out, gs, res)
+    )(*(pltpu.with_memory_space_constraint(v, pltpu.VMEM) for v in made))
     return output, grad_signal, gcw, gcb.reshape(-1), gow, gob.reshape(-1)
 
 

time: 72.9 us -> 57.6 us (0.79)
  local copies, waits for them, and re-layouts: 8.4 us -> 0 us
  Pallas kernels: 63.5 us -> 56.8 us
    unnamed x18 -> x0, local copies, waits for them, and re-layouts: 8.4 us -> none
    pallas_call x1, Pallas kernels: 59.3 us -> 54.6 us  [local(): pl.pallas_call(kernel, out_shape=(pltpu.VMEM((4 * B, B), BF), pltpu.VMEM(...]
    pallas_call x1, Pallas kernels: 4.12 us -> 2.19 us  [local(): pl.pallas_call(write_kernel, out_shape=(jax.ShapeDtypeStruct((1, 4 * B, B...]
where the time goes in v2:
time: 57.6 us; the launch traced here: 57.5 us
  Pallas kernels  56.8 us (99%)
  between operations  0.64 us (1%)
    pallas_call x1, Pallas kernels, local(): pl.pallas_call(kernel, out_shape=(pltpu.VMEM((4 * B, B), BF), pltpu.VMEM(...  54.6 us
    pallas_call x1, Pallas kernels, local(): pl.pallas_call(write_kernel, out_shape=(jax.ShapeDtypeStruct((1, 4 * B, B...  2.19 us

profile of v2, /device:TPU:1, one launch (start us, length us, event | category | flops | bytes accessed | tf_op | source)
XLA Modules:
  0.0 57.5 jit_solution(6398832967164389256)
XLA Ops:
  0.6 54.6 %block.1 = (bf16[1024,256]{1,0:T(8,128)(2,1)S(1)}, bf16[1024,256]{1,0:T(8,128)(2,1)S(1)}, f32[2,1024,256]{2,1,0:T(8,128)S(1)}) custom-call(bf16[1,1024,256]{2,1,0:T(8,128)(2,1)} %refs_0_.1, bf16[768,512]{1,0:T(8,128)(2,1)} %refs_1_.1, f32[1,512]{1,0:T(1,128)} %bitcast.4, bf16[256,256]{1,0:T(8,128)(2,1)} %refs_3_.1, f32[1,256]{1,0:T(1,128)} %bitcast.5, ...), custom_call_target="tpu_custom_call" | custom-call | tf_op jit(solution)/shard_map/block/pallas_call | solution.py:344
  55.3 2.2 %write.1 = (bf16[1,1024,256]{2,1,0:T(8,128)(2,1)}, bf16[1,1024,256]{2,1,0:T(8,128)(2,1)}, f32[768,512]{1,0:T(8,128)}, f32[1,512]{1,0:T(1,128)}, f32[256,256]{1,0:T(8,128)}, /*index=5*/f32[1,256]{1,0:T(1,128)}) custom-call(bf16[1024,256]{1,0:T(8,128)(2,1)S(1)} %get-tuple-element.15.out, bf16[1024,256]{1,0:T(8,128)(2,1)S(1)} %get-tuple-element.16.gs, ...), custom_call_target="tpu_custom_call" | custom-call | tf_op jit(solution)/shard_map/write/pallas_call | solution.py:390

commit v3 on v2

--- a/solution.py
+++ b/solution.py
@@ -14,6 +14,7 @@
 CH = 4
 PARTNERS = 32
 HI, LO = 128, 136
+USED = (32, 32, 32, 18)
 
 
 def nt(a, b):
@@ -45,9 +46,9 @@
     scale,
     sig, cw, cb, ow, ob, cot,
     out_ref, gs_ref, res_ref,
-    sx, cv, wv, owv, cbv, obv, mixed, dp, grad, gpart, bsend, binc,
+    sx, cv, wv, owv, cbv, obv, pre0, pre1, dmix, mixed, dp, grad, gpart, bsend, binc,
     sbuf, cbuf, acc, rbuf, part, agb, agc,
-    in_sem, halo_s, halo_r, back_s, back_r,
+    in_sem, known, halo_s, halo_r, back_s, back_r,
     cs, cr, rs, rr, ps, pr, gsem, gr, s2, r2,
 ):
     tm, run = lax.axis_index("tm"), lax.axis_index("run")
@@ -67,8 +68,8 @@
             zz, yy = rem(z + i, NZ), rem(y + i, NY)
             for j in range(first, NX):
                 xx = columns[j]
-                visit(0, i * NX + j, place(y, xx, zz, c), zz * NX + xx)
-                visit(1, i * NX + j, place(yy, xx, z, c), yy * NX + xx)
+                visit(0, i * NX + j, place(y, xx, zz, c), xx * 8 + zz)
+                visit(1, i * NX + j, place(yy, xx, z, c), xx * 8 + yy)
 
         def step(i, carry):
             line_of(i, 0)
@@ -77,7 +78,7 @@
         lax.fori_loop(1, 8, step, 0)
         line_of(0, 1)
 
-    mine = (z * 4 + x, y * 4 + x)
+    mine = (x * 8 + z, x * 8 + y)
     line = (y, z)
 
     def remote(src, dst, send, recv, device):
@@ -101,36 +102,41 @@
 
     barrier = pltpu.get_barrier_semaphore()
 
-    for device in (after, before, sibling):
-        pl.semaphore_signal(barrier, inc=1, device_id=device, device_id_type=MESH)
-    plane(lambda colour, slot, device, p: pl.semaphore_signal(barrier, inc=1, device_id=device, device_id_type=MESH))
-    pl.semaphore_wait(barrier, 2 * (PARTNERS - 1) + 3)
+    row = [place(y, columns[j], z, c) for j in range(1, NX)]
+    near = [along(colour, i) for i in (2, 6, 1, 7) for colour in range(2)] + row
+
+    def tell(semaphore, devices):
+        for device in devices:
+            pl.semaphore_signal(semaphore, inc=1, device_id=device, device_id_type=MESH)
+
+    tell(barrier, [after, before, *near, sibling])
+    pl.semaphore_wait(barrier, len(near) + 3)
     halos = []
     for i in (1, 0):
         src = sig.at[0, pl.ds((2 + i) * B, B)]
         copy = remote(src, sx.at[pl.ds(i * B, B)], halo_s.at[i], halo_r.at[i], after)
         copy.start()
         halos.append(copy)
+    tell(known.at[0], near)
     for load in loads:
         load.wait()
 
     def rows(b):
         return pl.ds(b * B, B)
 
-    def activate(b):
-        pre = (
-            nn(sx[(b + 2) * B : (b + 3) * B], wv[0:B])
-            + nn(sx[(b + 1) * B : (b + 2) * B], wv[B : 2 * B])
-            + nn(sx[b * B : (b + 1) * B], wv[2 * B : 3 * B])
-            + cbv[...]
-        )
+    def pre_term(b, k):
+        return nn(sx[(b + 2 - k) * B : (b + 3 - k) * B], wv[k * B : (k + 1) * B])
+
+    def activate(b, pre, dm):
         f = jnp.tanh(pre[:, :B])
         g = 0.5 * jnp.tanh(0.5 * pre[:, B:]) + 0.5
         mixed[rows(b), :] = (f * g).astype(BF)
-        dm = nt(cv[rows(b), :], owv[...])
         dmg = dm * g
         dp[rows(b), 0:B] = (dmg * (1.0 - f * f)).astype(BF)
         dp[rows(b), B : 2 * B] = (dmg * f * (1.0 - g)).astype(BF)
+
+    def mixed_back(b):
+        return nt(cv[rows(b), :], owv[...])
 
     def tap_term(k, b, n):
         return tn(sx[(b + 2 - k) * B : (b + 2 - k + n) * B], dp[b * B : (b + n) * B])
@@ -150,8 +156,10 @@
         h = nn(mixed[rows(b), :], owv[...]) + obv[...]
         out_ref[rows(b), :] = (sx[(b + 2) * B : (b + 3) * B].astype(F32) + h).astype(BF)
 
-    activate(2)
-    activate(3)
+    for b in (2, 3):
+        activate(b, pre_term(b, 0) + pre_term(b, 1) + pre_term(b, 2) + cbv[...], mixed_back(b))
+    pl.semaphore_wait(known.at[0], len(near))
+    tell(known.at[1], row)
     grad[:, 3, HI:B, :] = jnp.zeros((2, B - HI, B), F32)
     for k in range(3):
         t = tap_term(k, 2, 2)
@@ -165,6 +173,9 @@
     gpart[B : 2 * B, :] = cv[rows(3), :].astype(F32) + back(3, 0)
     emit_output(2)
     emit_output(3)
+    pre1[...] = pre_term(1, 0) + pre_term(1, 1) + cbv[...]
+    pre0[...] = pre_term(0, 0) + cbv[...]
+    dmix[...] = mixed_back(0)
 
     first = tm == 0
 
@@ -174,7 +185,8 @@
     def _():
         sx[B : 2 * B, :] = jnp.zeros((B, B), BF)
 
-    activate(1)
+    activate(1, pre1[...] + pre_term(1, 2), mixed_back(1))
+    pre0[...] += pre_term(0, 1)
     for k in range(3):
         t = tap_term(k, 1, 1)
         grad[0, k] += t[:, :B]
@@ -189,7 +201,7 @@
     def _():
         sx[0:B, :] = jnp.zeros((B, B), BF)
 
-    activate(0)
+    activate(0, pre0[...] + pre_term(0, 2), dmix[...])
     pair = []
 
     def send_half(k):
@@ -230,11 +242,18 @@
                 acc[k, colour, HI // 8] = high[:, colour * 128 : (colour + 1) * 128]
                 acc[k, colour, LO // 8] = low[:, colour * 128 : (colour + 1) * 128]
 
-        plane(
-            lambda colour, slot, device, p: remote(
-                acc.at[k, colour, p], rbuf.at[k, colour, slot], rs.at[k], rr.at[k, colour], device
-            ).start()
-        )
+        def scatter(colour, slot, device, p):
+            copy = remote(
+                acc.at[k, colour, p], rbuf.at[k, colour, slot], rs.at[k, colour], rr.at[k, colour], device
+            )
+            if USED[k] == PARTNERS:
+                copy.start()
+            else:
+                pl.when(p < USED[k])(copy.start)
+
+        if k == 0:
+            pl.semaphore_wait(known.at[1], NX - 1)
+        plane(scatter)
 
     bsend[0:B, :] = back(0, 2).astype(BF)
     bsend[B : 2 * B, :] = (back(0, 1) + back(1, 2)).astype(BF)
@@ -247,44 +266,71 @@
     emit_output(0)
     emit_output(1)
 
-    for k in range(CH):
-        for colour in range(2):
-            wait_bytes(rbuf.at[k, colour, pl.ds(1, PARTNERS - 1)], rr.at[k, colour])
-            s = acc[k, colour, mine[colour]].astype(F32)
-            s = s + jnp.sum(rbuf[k, colour, 1:PARTNERS].astype(F32), 0)
-            part[k, colour, line[colour]] = s
-
-            def spread(o, carry):
-                ref = part.at[k, colour, line[colour]]
-                remote(ref, ref, ps.at[k], pr.at[k, colour], along(colour, o)).start()
-                return carry
-
-            lax.fori_loop(1, 8, spread, 0)
+    def if_mine(k, colour, work):
+        if USED[k] == PARTNERS:
+            work()
+        else:
+            pl.when(mine[colour] < USED[k])(work)
+
+    def wait_others(k, colour, ref, sem):
+        n = USED[k]
+        if n == PARTNERS:
+            wait_bytes(ref.at[pl.ds(0, n - 1)], sem)
+        else:
+            pl.when(mine[colour] < n)(lambda: wait_bytes(ref.at[pl.ds(0, n - 1)], sem))
+            pl.when(mine[colour] >= n)(lambda: wait_bytes(ref.at[pl.ds(0, n)], sem))
+
+    for k in range(CH):
+        for colour in range(2):
+
+            def reduce_plane():
+                wait_bytes(rbuf.at[k, colour, pl.ds(1, PARTNERS - 1)], rr.at[k, colour])
+                s = acc[k, colour, mine[colour]].astype(F32)
+                s = s + jnp.sum(rbuf[k, colour, 1:PARTNERS].astype(F32), 0)
+                part[k, colour, line[colour]] = s
+
+                def spread(o, carry):
+                    ref = part.at[k, colour, line[colour]]
+                    remote(ref, ref, ps.at[k, colour], pr.at[k, colour], along(colour, o)).start()
+                    return carry
+
+                lax.fori_loop(1, 8, spread, 0)
+
+            if_mine(k, colour, reduce_plane)
         backward[k].start()
 
     for k in range(CH):
         for colour in range(2):
-            wait_bytes(part.at[k, colour, pl.ds(1, 7)], pr.at[k, colour])
-            t = part[k, colour, 0]
-            for i in range(1, 8):
-                t = t + part[k, colour, i]
-            agb[k, colour, mine[colour]] = t.astype(BF)
+
+            def finish():
+                wait_bytes(part.at[k, colour, pl.ds(1, 7)], pr.at[k, colour])
+                t = part[k, colour, 0]
+                for i in range(1, 8):
+                    t = t + part[k, colour, i]
+                agb[k, colour, mine[colour]] = t.astype(BF)
+
+            if_mine(k, colour, finish)
 
         def gather(colour, slot, device, p):
             ref = agb.at[k, colour, mine[colour]]
-            remote(ref, ref, gsem.at[k], gr.at[k, colour], device).start()
+            copy = remote(ref, ref, gsem.at[k, colour], gr.at[k, colour], device)
+            if_mine(k, colour, copy.start)
 
         plane(gather)
 
     def keep(h, k, colour, ref):
-        v = ref[k, colour].astype(F32).reshape(B, 128) * scale
-        res_ref[h, pl.ds(k * B, B), colour * 128 : (colour + 1) * 128] = v
+        n = USED[k]
+        v = ref[k, colour, 0:n].astype(F32).reshape(n * 8, 128) * scale
+        res_ref[h, pl.ds(k * B, n * 8), colour * 128 : (colour + 1) * 128] = v
 
     swap = []
     for k in range(CH):
-        for colour in range(2):
-            wait_bytes(agb.at[k, colour, pl.ds(1, PARTNERS - 1)], gr.at[k, colour])
-            copy = remote(agb.at[k, colour], agc.at[k, colour], s2.at[k, colour], r2.at[k, colour], sibling)
+        used = pl.ds(0, USED[k])
+        for colour in range(2):
+            wait_others(k, colour, agb.at[k, colour], gr.at[k, colour])
+            copy = remote(
+                agb.at[k, colour, used], agc.at[k, colour, used], s2.at[k, colour], r2.at[k, colour], sibling
+            )
             copy.start()
             swap.append(copy)
         for colour in range(2):
@@ -307,9 +353,14 @@
     for copy in (*halos, *pair, *backward, *swap):
         copy.wait_send()
     for k in range(CH):
-        wait_bytes(rbuf.at[k, :, pl.ds(1, PARTNERS - 1)], rs.at[k])
-        wait_bytes(part.at[k, :, pl.ds(1, 7)], ps.at[k])
-        wait_bytes(agb.at[k, :, pl.ds(1, PARTNERS - 1)], gsem.at[k])
+        for colour in range(2):
+            wait_others(k, colour, rbuf.at[k, colour], rs.at[k, colour])
+
+            def sent():
+                wait_bytes(part.at[k, colour, pl.ds(1, 7)], ps.at[k, colour])
+                wait_bytes(agb.at[k, colour, pl.ds(1, PARTNERS - 1)], gsem.at[k, colour])
+
+            if_mine(k, colour, sent)
 
 
 def write_kernel(out, gs, res, out_ref, gs_ref, gcw_ref, gcb_ref, gow_ref, gob_ref, sem):
@@ -353,6 +404,9 @@
             pltpu.VMEM((B, B), BF),
             pltpu.VMEM((1, 2 * B), F32),
             pltpu.VMEM((1, B), F32),
+            pltpu.VMEM((B, 2 * B), F32),
+            pltpu.VMEM((B, 2 * B), F32),
+            pltpu.VMEM((B, B), F32),
             pltpu.VMEM((4 * B, B), BF),
             pltpu.VMEM((4 * B, 2 * B), BF),
             pltpu.VMEM((2, CH, B, B), F32),
@@ -367,17 +421,18 @@
             pltpu.VMEM((CH, 2, PARTNERS, 8, 128), BF),
             pltpu.VMEM((CH, 2, PARTNERS, 8, 128), BF),
             dma((6,)),
+            pltpu.SemaphoreType.REGULAR((2,)),
             dma((2,)),
             dma((2,)),
             dma((CH,)),
             dma((CH,)),
             dma((CH,)),
             dma((CH,)),
-            dma((CH,)),
-            dma((CH, 2)),
-            dma((CH,)),
-            dma((CH, 2)),
-            dma((CH,)),
+            dma((CH, 2)),
+            dma((CH, 2)),
+            dma((CH, 2)),
+            dma((CH, 2)),
+            dma((CH, 2)),
             dma((CH, 2)),
             dma((CH, 2)),
             dma((CH, 2)),

time: 57.6 us -> 54.2 us (0.941)
  Pallas kernels: 56.8 us -> 53.4 us
    pallas_call x1, Pallas kernels: 54.6 us -> 51.2 us  [local(): pl.pallas_call(kernel, out_shape=(pltpu.VMEM((4 * B, B), BF), pltpu.VMEM(...]
where the time goes in v3:
time: 54.2 us; the launch traced here: 54 us
  Pallas kernels  53.4 us (99%)
  between operations  0.64 us (1%)
    pallas_call x1, Pallas kernels, local(): pl.pallas_call(kernel, out_shape=(pltpu.VMEM((4 * B, B), BF), pltpu.VMEM(...  51.2 us
    pallas_call x1, Pallas kernels, local(): pl.pallas_call(write_kernel, out_shape=(jax.ShapeDtypeStruct((1, 4 * B, B...  2.19 us

profile of v3, /device:TPU:1, one launch (start us, length us, event | category | flops | bytes accessed | tf_op | source)
XLA Modules:
  0.0 54.0 jit_solution(284463124369472503)
XLA Ops:
  0.6 51.2 %block.1 = (bf16[1024,256]{1,0:T(8,128)(2,1)S(1)}, bf16[1024,256]{1,0:T(8,128)(2,1)S(1)}, f32[2,1024,256]{2,1,0:T(8,128)S(1)}) custom-call(bf16[1,1024,256]{2,1,0:T(8,128)(2,1)} %refs_0_.1, bf16[768,512]{1,0:T(8,128)(2,1)} %refs_1_.1, f32[1,512]{1,0:T(1,128)} %bitcast.4, bf16[256,256]{1,0:T(8,128)(2,1)} %refs_3_.1, f32[1,256]{1,0:T(1,128)} %bitcast.5, ...), custom_call_target="tpu_custom_call" | custom-call | tf_op jit(solution)/shard_map/block/pallas_call | solution.py:395
  51.8 2.2 %write.1 = (bf16[1,1024,256]{2,1,0:T(8,128)(2,1)}, bf16[1,1024,256]{2,1,0:T(8,128)(2,1)}, f32[768,512]{1,0:T(8,128)}, f32[1,512]{1,0:T(1,128)}, f32[256,256]{1,0:T(8,128)}, /*index=5*/f32[1,256]{1,0:T(1,128)}) custom-call(bf16[1024,256]{1,0:T(8,128)(2,1)S(1)} %get-tuple-element.15.out, bf16[1024,256]{1,0:T(8,128)(2,1)S(1)} %get-tuple-element.16.gs, ...), custom_call_target="tpu_custom_call" | custom-call | tf_op jit(solution)/shard_map/write/pallas_call | solution.py:445

commit v4 on v3

--- a/solution.py
+++ b/solution.py
@@ -66,16 +66,16 @@
     def plane(visit):
         def line_of(i, first):
             zz, yy = rem(z + i, NZ), rem(y + i, NY)
-            for j in range(first, NX):
+            for j in (2, 1, 3, 0)[: NX - first]:
                 xx = columns[j]
                 visit(0, i * NX + j, place(y, xx, zz, c), xx * 8 + zz)
                 visit(1, i * NX + j, place(yy, xx, z, c), xx * 8 + yy)
 
-        def step(i, carry):
-            line_of(i, 0)
+        def step(t, carry):
+            line_of(4 + (2 * rem(t, 2) - 1) * div(t + 1, 2), 0)
             return carry
 
-        lax.fori_loop(1, 8, step, 0)
+        lax.fori_loop(0, 7, step, 0)
         line_of(0, 1)
 
     mine = (x * 8 + z, x * 8 + y)
@@ -297,7 +297,6 @@
                 lax.fori_loop(1, 8, spread, 0)
 
             if_mine(k, colour, reduce_plane)
-        backward[k].start()
 
     for k in range(CH):
         for colour in range(2):
@@ -317,13 +316,31 @@
             if_mine(k, colour, copy.start)
 
         plane(gather)
+    for copy in backward:
+        copy.start()
 
     def keep(h, k, colour, ref):
         n = USED[k]
         v = ref[k, colour, 0:n].astype(F32).reshape(n * 8, 128) * scale
         res_ref[h, pl.ds(k * B, n * 8), colour * 128 : (colour + 1) * 128] = v
 
+    def gathered(k, colour):
+        if_mine(k, colour, lambda: wait_bytes(agb.at[k, colour, pl.ds(1, PARTNERS - 1)], gsem.at[k, colour]))
+
+    for copy in (*halos, *pair):
+        copy.wait_send()
+    for k in range(CH):
+        for colour in range(2):
+            wait_others(k, colour, rbuf.at[k, colour], rs.at[k, colour])
+            if_mine(k, colour, lambda: wait_bytes(part.at[k, colour, pl.ds(1, 7)], ps.at[k, colour]))
+
     swap = []
+
+    def keep_other(k):
+        for colour in range(2):
+            swap[2 * k + colour].wait_recv()
+            keep(1 - c, k, colour, agc)
+
     for k in range(CH):
         used = pl.ds(0, USED[k])
         for colour in range(2):
@@ -335,6 +352,11 @@
             swap.append(copy)
         for colour in range(2):
             keep(c, k, colour, agb)
+            if k < CH - 1:
+                gathered(k, colour)
+        if k > 0:
+            keep_other(k - 1)
+    keep_other(CH - 1)
 
     for copy in backward:
         copy.wait_recv()
@@ -345,30 +367,18 @@
 
     for i in range(2):
         gs_ref[rows(2 + i), :] = (gpart[rows(i), :] + binc[rows(i), :].astype(F32)).astype(BF)
-    for k in range(CH):
-        for colour in range(2):
-            swap[2 * k + colour].wait_recv()
-            keep(1 - c, k, colour, agc)
-
-    for copy in (*halos, *pair, *backward, *swap):
+    for copy in (*backward, *swap):
         copy.wait_send()
-    for k in range(CH):
-        for colour in range(2):
-            wait_others(k, colour, rbuf.at[k, colour], rs.at[k, colour])
-
-            def sent():
-                wait_bytes(part.at[k, colour, pl.ds(1, 7)], ps.at[k, colour])
-                wait_bytes(agb.at[k, colour, pl.ds(1, PARTNERS - 1)], gsem.at[k, colour])
-
-            if_mine(k, colour, sent)
-
-
-def write_kernel(out, gs, res, out_ref, gs_ref, gcw_ref, gcb_ref, gow_ref, gob_ref, sem):
+    for colour in range(2):
+        gathered(CH - 1, colour)
+
+
+def write_kernel(out, gs, res, out_ref, gs_ref, gcw_ref, gcb_ref, gow_ref, gob_ref, cbias, obias, sem):
     copies = [
+        pltpu.make_async_copy(res.at[0, pl.ds(0, 768)], gcw_ref.at[:, pl.ds(0, B)], sem.at[2]),
+        pltpu.make_async_copy(res.at[1, pl.ds(0, 768)], gcw_ref.at[:, pl.ds(B, B)], sem.at[3]),
         pltpu.make_async_copy(out, out_ref.at[0], sem.at[0]),
         pltpu.make_async_copy(gs, gs_ref.at[0], sem.at[1]),
-        pltpu.make_async_copy(res.at[0, pl.ds(0, 768)], gcw_ref.at[:, pl.ds(0, B)], sem.at[2]),
-        pltpu.make_async_copy(res.at[1, pl.ds(0, 768)], gcw_ref.at[:, pl.ds(B, B)], sem.at[3]),
         pltpu.make_async_copy(res.at[0, pl.ds(768, 128)], gow_ref.at[pl.ds(0, 128)], sem.at[4]),
         pltpu.make_async_copy(res.at[1, pl.ds(768, 128)], gow_ref.at[pl.ds(128, 128)], sem.at[5]),
     ]
@@ -376,9 +386,15 @@
         copy.start()
     hi, lo = 768 + HI, 768 + LO
     for h in range(2):
-        gcb_ref[0:1, h * B : (h + 1) * B] = res[h, hi : hi + 1, :] + res[h, lo : lo + 1, :]
-    gob_ref[...] = res[0, hi + 1 : hi + 2, :] + res[0, lo + 1 : lo + 2, :]
-    for copy in copies:
+        cbias[0:1, h * B : (h + 1) * B] = res[h, hi : hi + 1, :] + res[h, lo : lo + 1, :]
+    obias[...] = res[0, hi + 1 : hi + 2, :] + res[0, lo + 1 : lo + 2, :]
+    small = [
+        pltpu.make_async_copy(cbias, gcb_ref, sem.at[6]),
+        pltpu.make_async_copy(obias, gob_ref, sem.at[7]),
+    ]
+    for copy in small:
+        copy.start()
+    for copy in copies + small:
         copy.wait()
 
 
@@ -453,8 +469,8 @@
             jax.ShapeDtypeStruct((1, B), F32),
         ),
         in_specs=[vmem] * 3,
-        out_specs=[any_space, any_space, any_space, vmem, any_space, vmem],
-        scratch_shapes=[dma((6,))],
+        out_specs=[any_space] * 6,
+        scratch_shapes=[pltpu.VMEM((1, 2 * B), F32), pltpu.VMEM((1, B), F32), dma((8,))],
         name="write",
     )(*(pltpu.with_memory_space_constraint(v, pltpu.VMEM) for v in made))
     return output, grad_signal, gcw, gcb.reshape(-1), gow, gob.reshape(-1)

time: 54.2 us -> 51.8 us (0.956); the launches traced: 54 us -> 50.8 us
  Pallas kernels: 53.4 us -> 50.2 us
    pallas_call x1, Pallas kernels: 51.2 us -> 48.5 us  [local(): pl.pallas_call(kernel, out_shape=(pltpu.VMEM((4 * B, B), BF), pltpu.VMEM(...]
    pallas_call x1, Pallas kernels: 2.19 us -> 1.64 us  [local(): pl.pallas_call(write_kernel, out_shape=(jax.ShapeDtypeStruct((1, 4 * B, B...]
where the time goes in v4:
time: 51.8 us; the launch traced here: 50.8 us
  Pallas kernels  50.2 us (97%)
  between operations  0.64 us (1%)
    pallas_call x1, Pallas kernels, local(): pl.pallas_call(kernel, out_shape=(pltpu.VMEM((4 * B, B), BF), pltpu.VMEM(...  48.5 us
    pallas_call x1, Pallas kernels, local(): pl.pallas_call(write_kernel, out_shape=(jax.ShapeDtypeStruct((1, 4 * B, B...  1.64 us

profile of v4, /device:TPU:1, one launch (start us, length us, event | category | flops | bytes accessed | tf_op | source)
XLA Modules:
  0.0 50.8 jit_solution(604965482940993770)
XLA Ops:
  0.6 48.5 %block.1 = (bf16[1024,256]{1,0:T(8,128)(2,1)S(1)}, bf16[1024,256]{1,0:T(8,128)(2,1)S(1)}, f32[2,1024,256]{2,1,0:T(8,128)S(1)}) custom-call(bf16[1,1024,256]{2,1,0:T(8,128)(2,1)} %refs_0_.1, bf16[768,512]{1,0:T(8,128)(2,1)} %refs_1_.1, f32[1,512]{1,0:T(1,128)} %bitcast.4, bf16[256,256]{1,0:T(8,128)(2,1)} %refs_3_.1, f32[1,256]{1,0:T(1,128)} %bitcast.5, ...), custom_call_target="tpu_custom_call" | custom-call | tf_op jit(solution)/shard_map/block/pallas_call | solution.py:411
  49.2 1.6 %write.1 = (bf16[1,1024,256]{2,1,0:T(8,128)(2,1)}, bf16[1,1024,256]{2,1,0:T(8,128)(2,1)}, f32[768,512]{1,0:T(8,128)}, f32[1,512]{1,0:T(1,128)}, f32[256,256]{1,0:T(8,128)}, /*index=5*/f32[1,256]{1,0:T(1,128)}) custom-call(bf16[1024,256]{1,0:T(8,128)(2,1)S(1)} %get-tuple-element.15.out, bf16[1024,256]{1,0:T(8,128)(2,1)S(1)} %get-tuple-element.16.gs, ...), custom_call_target="tpu_custom_call" | custom-call | tf_op jit(solution)/shard_map/write/pallas_call | solution.py:461

commit v5 on v4

--- a/solution.py
+++ b/solution.py
@@ -169,10 +169,6 @@
     grad[0, 3, 0:HI, :] = t[:HI]
     grad[1, 3, 0:HI, :] = t[HI:]
     d23, o23 = bias_terms(2, 2)
-    gpart[0:B, :] = cv[rows(2), :].astype(F32) + back(2, 0) + back(3, 1)
-    gpart[B : 2 * B, :] = cv[rows(3), :].astype(F32) + back(3, 0)
-    emit_output(2)
-    emit_output(3)
     pre1[...] = pre_term(1, 0) + pre_term(1, 1) + cbv[...]
     pre0[...] = pre_term(0, 0) + cbv[...]
     dmix[...] = mixed_back(0)
@@ -195,6 +191,8 @@
     grad[0, 3, 0:HI, :] += t[:HI]
     grad[1, 3, 0:HI, :] += t[HI:]
 
+    d1, o1 = bias_terms(1, 1)
+
     halos[1].wait_recv()
 
     @pl.when(first)
@@ -218,8 +216,8 @@
     t = out_term(0, 1)
     grad[0, 3, 0:HI, :] += t[:HI]
     grad[1, 3, 0:HI, :] += t[HI:]
-    d01, o01 = bias_terms(0, 2)
-    d, o = d23 + d01, o23 + o01
+    d0, o0 = bias_terms(0, 1)
+    d, o = d23 + d1 + d0, o23 + o1 + o0
     for h in range(2):
         grad[h, 3, HI : HI + 1, :] = d[:, h * B : (h + 1) * B]
         grad[h, 3, HI + 1 : HI + 2, :] = o
@@ -265,6 +263,10 @@
     gs_ref[rows(1), :] = (cv[rows(1), :].astype(F32) + back(1, 0) + back(2, 1) + back(3, 2)).astype(BF)
     emit_output(0)
     emit_output(1)
+    gpart[0:B, :] = cv[rows(2), :].astype(F32) + back(2, 0) + back(3, 1)
+    gpart[B : 2 * B, :] = cv[rows(3), :].astype(F32) + back(3, 0)
+    emit_output(2)
+    emit_output(3)
 
     def if_mine(k, colour, work):
         if USED[k] == PARTNERS:

time: 51.8 us -> 51.7 us (level); the launches traced: 50.8 us -> 51.2 us
  no operation moved by 1% of the time
where the time goes in v5:
time: 51.7 us; the launch traced here: 51.2 us
  Pallas kernels  50.6 us (98%)
  between operations  0.64 us (1%)
    pallas_call x1, Pallas kernels, local(): pl.pallas_call(kernel, out_shape=(pltpu.VMEM((4 * B, B), BF), pltpu.VMEM(...  49 us
    pallas_call x1, Pallas kernels, local(): pl.pallas_call(write_kernel, out_shape=(jax.ShapeDtypeStruct((1, 4 * B, B...  1.64 us

profile of v5, /device:TPU:1, one launch (start us, length us, event | category | flops | bytes accessed | tf_op | source)
XLA Modules:
  0.0 51.2 jit_solution(16881564390289339016)
XLA Ops:
  0.6 49.0 %block.1 = (bf16[1024,256]{1,0:T(8,128)(2,1)S(1)}, bf16[1024,256]{1,0:T(8,128)(2,1)S(1)}, f32[2,1024,256]{2,1,0:T(8,128)S(1)}) custom-call(bf16[1,1024,256]{2,1,0:T(8,128)(2,1)} %refs_0_.1, bf16[768,512]{1,0:T(8,128)(2,1)} %refs_1_.1, f32[1,512]{1,0:T(1,128)} %bitcast.4, bf16[256,256]{1,0:T(8,128)(2,1)} %refs_3_.1, f32[1,256]{1,0:T(1,128)} %bitcast.5, ...), custom_call_target="tpu_custom_call" | custom-call | tf_op jit(solution)/shard_map/block/pallas_call | solution.py:413
  49.6 1.6 %write.1 = (bf16[1,1024,256]{2,1,0:T(8,128)(2,1)}, bf16[1,1024,256]{2,1,0:T(8,128)(2,1)}, f32[768,512]{1,0:T(8,128)}, f32[1,512]{1,0:T(1,128)}, f32[256,256]{1,0:T(8,128)}, /*index=5*/f32[1,256]{1,0:T(1,128)}) custom-call(bf16[1024,256]{1,0:T(8,128)(2,1)S(1)} %get-tuple-element.15.out, bf16[1024,256]{1,0:T(8,128)(2,1)S(1)} %get-tuple-element.16.gs, ...), custom_call_target="tpu_custom_call" | custom-call | tf_op jit(solution)/shard_map/write/pallas_call | solution.py:463
